TPU v7x, 128 devices: a whole 4x4x4 slice. The times are simulated.
128 devices in a mesh: row: 16 (over x, z), col: 8 (over y, core).
Axes of the slice: x: 4, y: 4, z: 4, core: 2. Of those that a mesh axis runs over, the one named last changes fastest.
Arguments:
- trailing: bfloat16 [49152, 16384], P('row', 'col'), may hold values from -6 to 6
- panels: bfloat16 [2, 256, 49152], P(None, 'col', 'row'), as said below
- diag_lower: bfloat16 [2, 256, 256], P(None, 'col'), as said below
- pivot_src: int32 [2, 256], replicated, may hold values from 0 to 49151, as said below
- pivot_dst: int32 [2, 256], replicated, may hold values from 256 to 49152, as said below
Outputs:
- matrix: bfloat16 [49152, 16384], P('row', 'col')
Inputs may be any that keep to these rules, and one draw needn't show every extreme that they name: The entries of pivot_src[k] are distinct rows, none below 256 * k. Entries of pivot_dst[k] under 49152 are distinct, not below 256 * (k + 1), and are exactly the entries of pivot_src[k] that are not below 256 * (k + 1); an entry equal to 49152 marks an old row t + j that is itself one of pivot_src[k]. panels[k, c, r] is zero for r < 256 * (k + 1). diag_lower[k, r, c] is zero for c >= r.
All inputs are finite; a program needn't handle non-finite values.
Results may differ from a plain program's by a relative error of at most 0.0062.
Values may be sent and summed in bfloat16 or wider, within the bound.
No kernel may reach another device: no remote copies, remote signals or barrier semaphores. Data moves between devices by JAX's collectives and lax.ppermute only.
A program may use at most 128 MiB of HBM per device.

v0:
```python
import jax
import jax.numpy as jnp
from jax import lax
from jax.sharding import PartitionSpec as P


def broadcast(x, axis, root):
    mine = lax.axis_index(axis) == root
    return lax.psum(jnp.where(mine, x, jnp.zeros_like(x)), axis)


def per_device(trailing, panels, diag_lower, pivot_src, pivot_dst):
    rows_dev, cols_dev = trailing.shape
    panel_width = diag_lower.shape[2]
    row_index = lax.axis_index("row")
    offset = row_index * rows_dev
    identity = jnp.eye(panel_width, dtype=jnp.float32)
    matrix = trailing
    for panel_step in range(pivot_src.shape[0]):
        start_row = panel_step * panel_width
        sources = pivot_src[panel_step] - offset
        holding = (sources >= 0) & (sources < rows_dev)
        picked = jnp.take(matrix, jnp.clip(sources, 0, rows_dev - 1), axis=0)
        picked = jnp.where(holding[:, None], picked, jnp.zeros((), jnp.bfloat16))
        top_rows = matrix[start_row : start_row + panel_width]
        displaced = broadcast(top_rows, "row", 0)
        targets = pivot_dst[panel_step] - offset
        targets = jnp.where((targets >= 0) & (targets < rows_dev), targets, rows_dev)
        swapped = matrix.at[targets].set(displaced, mode="drop")
        factor = lax.all_gather(diag_lower[panel_step], "col", axis=0, tiled=True)
        unit_lower = factor.astype(jnp.float32) + identity
        block_rows = lax.psum(picked, "row").astype(jnp.float32)
        upper_rows = jax.scipy.linalg.solve_triangular(
            unit_lower, block_rows, lower=True, unit_diagonal=True
        ).astype(jnp.bfloat16)
        product = lax.dot_general(
            lax.all_gather(panels[panel_step], "col", axis=0, tiled=True),
            upper_rows,
            (((0,), (0,)), ((), ())),
            preferred_element_type=jnp.float32,
        )
        result = (swapped.astype(jnp.float32) - product).astype(jnp.bfloat16)
        current = result[start_row : start_row + panel_width]
        matrix = result.at[start_row : start_row + panel_width].set(
            jnp.where(row_index == 0, upper_rows, current)
        )
    return matrix


def solution(mesh):
    placed = (P("row", "col"), P(None, "col", "row"), P(None, "col", None), P(), P())
    return jax.shard_map(
        per_device, mesh=mesh, in_specs=placed, out_specs=P("row", "col"), check_vma=False
    )
```

profile of v0, /device:TPU:0, one launch (start us, length us, event | category | flops | bytes accessed | tf_op | source)
XLA Modules:
  0.0 298.3 jit_solution(11988537814029890667)
XLA Ops:
  7.4 0.0 copy-start.3
  7.4 0.0 all-reduce.7.cloned.1.call-start
  7.4 10.7 %copy.35 = bf16[3072,2048]{1,0:T(8,128)(2,1)} copy(bf16[3072,2048]{1,0:T(8,128)(2,1)} %param.13) | data formatting | bytes 25165824
  18.1 0.0 copy-start.1
  18.1 0.0 copy-start.2
  18.1 0.0 copy-start.4
  18.1 0.0 copy-done.3
  18.2 8.6 %gather_fusion = bf16[256,2048]{1,0:T(8,128)(2,1)S(1)} fusion(bf16[3072,2048]{1,0:T(8,128)(2,1)} %copy.35, s32[1024]{0:T(1024)S(1)} %pad_clamp_fusion.1), kind=kCustom, calls=%fused_computation.clone | custom fusion | bytes 2098176 | tf_op jit(solution)/shard_map/jit(_take)/gather | solution.py:23
  26.8 2.8 select_select_fusion.1
  29.7 0.0 all-reduce.7.cloned.1.call-update
  29.7 0.0 all-gather.7.cloned.1.call-start
  29.7 0.0 copy-done.1
  29.7 0.8 fusion.20
  30.5 0.0 all-gather.7.cloned.1.call-update
  30.5 0.0 all-reduce.5.cloned.1.call-start
  30.6 0.0 copy-done.2
  30.6 13.4 %all-gather = bf16[1,256,256]{2,1,0:T(8,128)(2,1)S(1)} all-gather(bf16[1,32,256]{2,1,0:T(8,128)(2,1)S(1)} %get-tuple-element.76), channel_id=2, replica_groups=mesh['row'=16,'col'=8] {'col'}, dimensions={1}, use_global_device_ids=true | all-gather | bytes 147456 | tf_op jit(solution)/shard_map/all_gather | solution.py:30
  44.0 13.0 %all-gather.2 = bf16[1,256,256]{2,1,0:T(8,128)(2,1)S(1)} all-gather(bf16[1,32,256]{2,1,0:T(8,128)(2,1)S(1)} %get-tuple-element.75), channel_id=4, replica_groups=mesh['row'=16,'col'=8] {'col'}, dimensions={1}, use_global_device_ids=true | all-gather | bytes 147456 | tf_op jit(solution)/shard_map/all_gather | solution.py:30
  57.0 0.1 convert_add_fusion
  57.1 0.1 triangular_solve.107
  57.2 4.3 %while.6 = (s32[]{:T(128)}, f32[256,256]{1,0:T(8,128)S(1)}, s32[2,2]{1,0:T(2,128)S(1)}, f32[2,128,128]{2,1,0:T(8,128)S(1)}, s32[]{:T(128)}) while((s32[]{:T(128)}, f32[256,256]{1,0:T(8,128)S(1)}, s32[2,2]{1,0:T(2,128)S(1)}, f32[2,128,128]{2,1,0:T(8,128)S(1)}, s32[]{:T(128)}) %tuple.51), condition=%wide.while_cond.2, body=%wide.while_body.2.sunk | while | flops 2 | bytes 131181 | solution.py:33
  57.3 0.7 fusion.28
  57.9 1.5 bitcast_dynamic-update-slice_fusion.4
  59.4 0.7 fusion.28
  60.1 1.5 bitcast_dynamic-update-slice_fusion.4
  61.6 0.0 copy-start
  61.6 0.0 copy-start.5
  61.6 19.7 %custom-call.4 = f32[2,128,128]{1,2,0:T(8,128)S(1)} custom-call(f32[2,128,128]{2,1,0:T(8,128)S(1)} %get-tuple-element.45), custom_call_target="InvertDiagBlocksLowerTriangular" | custom-call | tf_op jit(solution)/shard_map/jit(_solve_triangular)/triangular_solve | solution.py:33
  81.3 0.0 copy-done.4
  81.3 41.8 %all-reduce.7.cloned.1.call-done = (bf16[256,2048]{1,0:T(8,128)(2,1)}, bf16[256,2048]{1,0:T(8,128)(2,1)}) async-done(((bf16[256,2048]{1,0:T(8,128)(2,1)}, bf16[256,2048]{1,0:T(8,128)(2,1)}), (bf16[256,2048]{1,0:T(8,128)(2,1)}, bf16[256,2048]{1,0:T(8,128)(2,1)})) %all-reduce.7.cloned.1.call-update) | async-done | bytes 2097168 | tf_op jit(solution)/shard_map/psum | solution.py:9
  123.1 0.0 copy-done
  123.1 0.0 copy-done.5
  123.1 1.5 convert_element_type.38
  124.6 15.3 %scatter_fusion = bf16[3072,2048]{1,0:T(8,128)(2,1)} fusion(bf16[3072,2048]{1,0:T(8,128)(2,1)} %copy.35, s32[256]{0:T(256)S(1)} %bitcast.65, bf16[256,2048]{1,0:T(8,128)(2,1)} %get-tuple-element.67), kind=kCustom, calls=%fused_computation.2 | custom fusion | bytes 3146752 | tf_op jit(solution)/shard_map/scatter | solution.py:29
  139.9 1.1 fusion.8
  140.9 1.9 convolution_subtract_fusion.1
  142.8 1.1 fusion.15
  143.9 0.0 all-gather.7.cloned.1.call-done
  143.9 9.9 %fusion.1 = bf16[3072,2048]{1,0:T(8,128)(2,1)} fusion(bf16[3072,2048]{1,0:T(8,128)(2,1)} %scatter_fusion, bf16[1,256,3072]{2,1,0:T(8,128)(2,1)} %all-gather.7.cloned.1.call-done, bf16[128,2048]{1,0:T(8,128)(2,1)S(1)} %fusion.15, f32[128,2048]{1,0:T(8,128)S(1)} %fusion.8), kind=kOutput, calls=%fused_computation.11 | convolution fusion | flops 3242196992 | bytes 28311552 | tf_op jit(solution)/shard_map/dot_general | solution.py:36
  153.8 0.0 copy-start.6
  153.8 2.5 fusion.7
  156.3 2.3 slice_select_fusion.1
  158.6 8.6 %gather_fusion.1 = bf16[256,2048]{1,0:T(8,128)(2,1)S(1)} fusion(bf16[3072,2048]{1,0:T(8,128)(2,1)} %fusion.7, s32[1024]{0:T(1024)S(1)} %pad_clamp_fusion), kind=kCustom, calls=%fused_computation.1.clone | custom fusion | bytes 2098176 | tf_op jit(solution)/shard_map/jit(_take)/gather | solution.py:23
  167.2 1.2 select_select_fusion
  168.4 0.0 all-reduce.5.cloned.1.call-update
  168.4 0.2 all-gather.9.cloned.1.call-start
  168.6 0.4 all-gather.9.cloned.1.call-update
  169.0 0.0 copy-done.6
  169.0 3.8 %while.7 = (s32[]{:T(128)}, f32[256,256]{1,0:T(8,128)S(1)}, s32[2,2]{1,0:T(2,128)S(1)}, f32[2,128,128]{2,1,0:T(8,128)S(1)}, s32[]{:T(128)}) while((s32[]{:T(128)}, f32[256,256]{1,0:T(8,128)S(1)}, s32[2,2]{1,0:T(2,128)S(1)}, f32[2,128,128]{2,1,0:T(8,128)S(1)}, s32[]{:T(128)}) %tuple.67), condition=%wide.while_cond.2.clone, body=%wide.while_body.2.clone.sunk | while | flops 2 | bytes 131181 | solution.py:33
  169.0 0.6 fusion.29
  169.6 1.3 bitcast_dynamic-update-slice_fusion.5
  170.9 0.6 fusion.29
  171.5 1.3 bitcast_dynamic-update-slice_fusion.5
  172.8 19.7 %custom-call.5 = f32[2,128,128]{1,2,0:T(8,128)S(1)} custom-call(f32[2,128,128]{2,1,0:T(8,128)S(1)} %get-tuple-element.46), custom_call_target="InvertDiagBlocksLowerTriangular" | custom-call | tf_op jit(solution)/shard_map/jit(_solve_triangular)/triangular_solve | solution.py:33
  192.5 66.2 %all-reduce.5.cloned.1.call-done = (bf16[256,2048]{1,0:T(8,128)(2,1)}, bf16[256,2048]{1,0:T(8,128)(2,1)}) async-done(((bf16[256,2048]{1,0:T(8,128)(2,1)}, bf16[256,2048]{1,0:T(8,128)(2,1)}), (bf16[256,2048]{1,0:T(8,128)(2,1)}, bf16[256,2048]{1,0:T(8,128)(2,1)})) %all-reduce.5.cloned.1.call-update) | async-done | bytes 2097168 | tf_op jit(solution)/shard_map/psum | solution.py:9
  258.6 1.5 convert_element_type.43
  260.1 15.0 %scatter_fusion.1 = bf16[3072,2048]{1,0:T(8,128)(2,1)} fusion(bf16[3072,2048]{1,0:T(8,128)(2,1)} %fusion.7, s32[256]{0:T(256)S(1)} %bitcast.64, bf16[256,2048]{1,0:T(8,128)(2,1)} %get-tuple-element.65), kind=kCustom, calls=%fused_computation.3 | custom fusion | bytes 3146752 | tf_op jit(solution)/shard_map/scatter | solution.py:29
  275.1 1.1 fusion.5
  276.1 1.0 convolution_subtract_fusion
  277.2 1.1 fusion.13
  278.2 0.0 all-gather.9.cloned.1.call-done
  278.3 9.9 %fusion = bf16[3072,2048]{1,0:T(8,128)(2,1)} fusion(bf16[3072,2048]{1,0:T(8,128)(2,1)} %scatter_fusion.1, bf16[1,256,3072]{2,1,0:T(8,128)(2,1)} %all-gather.9.cloned.1.call-done, bf16[128,2048]{1,0:T(8,128)(2,1)S(1)} %fusion.13, f32[128,2048]{1,0:T(8,128)S(1)} %fusion.5), kind=kOutput, calls=%fused_computation.9 | convolution fusion | flops 3242196992 | bytes 28311552 | tf_op jit(solution)/shard_map/dot_general | solution.py:36
  288.1 2.5 fusion.4
  (18 shorter events, 0.1 us)
Async XLA Ops:
  7.4 10.7 %copy-start.3 = (s32[2,256]{1,0:T(2,128)S(1)}, s32[2,256]{1,0:T(2,128)}, u32[]{:S(2)}) copy-start(s32[2,256]{1,0:T(2,128)} %param.16) | copy-start | bytes 6148
  7.4 115.7 %all-reduce.7.cloned.1.call-start = ((), (), s32[]{:S(2)}) async-start(), calls=%async_computation.3 | async-start | bytes 4194304 | tf_op jit(solution)/shard_map/psum | solution.py:9
  18.1 11.6 %copy-start.1 = (bf16[2,32,3072]{2,1,0:T(8,128)(2,1)S(1)}, bf16[2,32,3072]{2,1,0:T(8,128)(2,1)}, u32[]{:S(2)}) copy-start(bf16[2,32,3072]{2,1,0:T(8,128)(2,1)} %param.14) | copy-start | bytes 1179652
  18.1 12.5 %copy-start.2 = (bf16[2,32,256]{2,1,0:T(8,128)(2,1)S(1)}, bf16[2,32,256]{2,1,0:T(8,128)(2,1)}, u32[]{:S(2)}) copy-start(bf16[2,32,256]{2,1,0:T(8,128)(2,1)} %param.15) | copy-start | bytes 98308
  18.1 63.2 %copy-start.4 = (s32[2,256]{1,0:T(2,128)S(1)}, s32[2,256]{1,0:T(2,128)}, u32[]{:S(2)}) copy-start(s32[2,256]{1,0:T(2,128)} %param.17) | copy-start | bytes 6148
  29.7 114.2 %all-gather.7.cloned.1.call-start = ((), (), s32[]{:S(2)}) async-start(), calls=%async_computation | async-start | bytes 1769472 | tf_op jit(solution)/shard_map/all_gather | solution.py:37
  30.5 228.1 %all-reduce.5.cloned.1.call-start = ((), (), s32[]{:S(2)}) async-start(), calls=%async_computation.2 | async-start | bytes 4194304 | tf_op jit(solution)/shard_map/psum | solution.py:9
  61.6 61.5 %copy-start = (f32[256,256]{1,0:T(8,128)}, f32[256,256]{1,0:T(8,128)S(1)}, u32[]{:S(2)}) copy-start(f32[256,256]{1,0:T(8,128)S(1)} %get-tuple-element.190) | copy-start | bytes 786436
  61.6 61.5 %copy-start.5 = (s32[2,2]{1,0:T(2,128)}, s32[2,2]{1,0:T(2,128)S(1)}, u32[]{:S(2)}) copy-start(s32[2,2]{1,0:T(2,128)S(1)} %get-tuple-element.203) | copy-start | bytes 52
  153.8 15.2 %copy-start.6 = (s32[2,2]{1,0:T(2,128)S(1)}, s32[2,2]{1,0:T(2,128)}, u32[]{:S(2)}) copy-start(s32[2,2]{1,0:T(2,128)} %copy-done.5) | copy-start | bytes 52
  168.4 109.9 %all-gather.9.cloned.1.call-start = ((), (), s32[]{:S(2)}) async-start(), calls=%async_computation.1 | async-start | bytes 1769472 | tf_op jit(solution)/shard_map/all_gather | solution.py:37
Sparse Core Ops, SparseCore 0:
  29.8 93.2 all-reduce.6
  168.5 90.0 all-reduce.4
Sparse Core Ops, SparseCore 1:
  31.9 26.9 all-gather.6
  170.6 23.8 all-gather.8
where the time goes:
time: 303 us; the launch traced here: 298 us
  waiting for transfers between devices  108 us (36%)
  local copies, waits for them, and re-layouts  67.1 us (22%)
  other arithmetic  53.9 us (18%)
  matrix products  26.8 us (9%)
  blocking collectives  26.4 us (9%)
  between operations  15.4 us (5%)
    psum x2, waiting for transfers between devices, broadcast(): return lax.psum(jnp.where(mine, x, jnp.zeros_like(x)), axis)  108 us
    another operation x5, other arithmetic, per_device(): jax.scipy.linalg.solve_triangular(unit_lower, block_rows, lower=True, uni...  39.5 us
    scatter x2, local copies, waits for them, and re-layouts, per_device(): swapped = matrix.at[targets].set(displaced, mode='drop')  30.3 us
    all_gather x2, blocking collectives, per_device(): factor = lax.all_gather(diag_lower[panel_step], 'col', axis=0, tiled=True)  26.4 us
    dot_general x2, matrix products, per_device(): lax.dot_general(lax.all_gather(panels[panel_step], 'col', axis=0, tiled=T...  19.8 us
    gather x2, local copies, waits for them, and re-layouts, per_device(): picked = jnp.take(matrix, jnp.clip(sources, 0, rows_dev - 1), axis=0)  17.2 us
    unnamed x15, local copies, waits for them, and re-layouts  10.8 us
    another operation x15, local copies, waits for them, and re-layouts, per_device(): jax.scipy.linalg.solve_triangular(unit_lower, block_rows, lower=True, uni...  8.1 us
  transfers between devices with their start and end apart: 4, of which 2 were waited for; matrix products, arithmetic and copies ran while one was open for 30% of the time, Pallas kernels for 0%

commit v1 on v0

--- a/solution.py
+++ b/solution.py
@@ -2,11 +2,18 @@
 import jax.numpy as jnp
 from jax import lax
 from jax.sharding import PartitionSpec as P
+from jax.lax import all_gather
+
+
+def guide_tiles_over_axis(local, mesh_ax):
+    state_next = all_gather(local, mesh_ax)
+    carry = jnp.sum(state_next, axis=0)
+    return carry
 
 
 def broadcast(x, axis, root):
     mine = lax.axis_index(axis) == root
-    return lax.psum(jnp.where(mine, x, jnp.zeros_like(x)), axis)
+    return guide_tiles_over_axis(jnp.where(mine, x, jnp.zeros_like(x)), axis)
 
 
 def per_device(trailing, panels, diag_lower, pivot_src, pivot_dst):

time: 303 us -> 529 us (1.75)
  waiting for transfers between devices: 108 us -> 317 us
  other arithmetic: 53.9 us -> 73.1 us
    all_gather x0 -> x2, waiting for transfers between devices: none -> 216 us  [guide_tiles_over_axis(): state_next = all_gather(local, mesh_ax)]
    reduce_sum x0 -> x2, other arithmetic: none -> 18.5 us  [guide_tiles_over_axis(): carry = jnp.sum(state_next, axis=0)]
    psum x2, waiting for transfers between devices: 108 us -> 97.2 us  [per_device(): block_rows = lax.psum(picked, 'row').astype(jnp.float32)]
    unnamed x15 -> x9, local copies, waits for them, and re-layouts: 10.8 us -> 10.7 us
  transfers between devices with their start and end apart: 4 -> 6, of which waited for: 2 -> 6; matrix products, arithmetic and copies ran while one was open for 30% -> 21% of each run, Pallas kernels for 0% -> 0%
where the time goes in v1:
time: 529 us; the launch traced here: 523 us
  waiting for transfers between devices  317 us (60%)
  other arithmetic  73.1 us (14%)
  local copies, waits for them, and re-layouts  65.7 us (12%)
  blocking collectives  26.6 us (5%)
  matrix products  26 us (5%)
  between operations  14 us (3%)
    all_gather x2, waiting for transfers between devices, guide_tiles_over_axis(): state_next = all_gather(local, mesh_ax)  216 us
    psum x2, waiting for transfers between devices, per_device(): block_rows = lax.psum(picked, 'row').astype(jnp.float32)  97.2 us
    another operation x5, other arithmetic, per_device(): jax.scipy.linalg.solve_triangular(unit_lower, block_rows, lower=True, uni...  39.5 us
    scatter x2, local copies, waits for them, and re-layouts, per_device(): swapped = matrix.at[targets].set(displaced, mode='drop')  29.1 us
    all_gather x2, blocking collectives, per_device(): factor = lax.all_gather(diag_lower[panel_step], 'col', axis=0, tiled=True)  26.6 us
    dot_general x2, matrix products, per_device(): lax.dot_general(lax.all_gather(panels[panel_step], 'col', axis=0, tiled=T...  19.7 us
    reduce_sum x2, other arithmetic, guide_tiles_over_axis(): carry = jnp.sum(state_next, axis=0)  18.5 us
    gather x2, local copies, waits for them, and re-layouts, per_device(): picked = jnp.take(matrix, jnp.clip(sources, 0, rows_dev - 1), axis=0)  17.2 us
  transfers between devices with their start and end apart: 6, of which 6 were waited for; matrix products, arithmetic and copies ran while one was open for 21% of the time, Pallas kernels for 0%

profile of v1, /device:TPU:0, one launch (start us, length us, event | category | flops | bytes accessed | tf_op | source)
XLA Modules:
  0.0 523.2 jit_solution(830308207915799835)
XLA Ops:
  6.5 0.0 copy-start.2
  6.5 0.0 all-reduce.3.cloned.1.call-start
  6.5 10.7 %copy.33 = bf16[3072,2048]{1,0:T(8,128)(2,1)} copy(bf16[3072,2048]{1,0:T(8,128)(2,1)} %param.13) | data formatting | bytes 25165824
  17.3 0.0 copy-start
  17.3 0.0 copy-done.2
  17.4 8.6 %gather_fusion = bf16[256,2048]{1,0:T(8,128)(2,1)S(1)} fusion(bf16[3072,2048]{1,0:T(8,128)(2,1)} %copy.33, s32[1024]{0:T(1024)S(1)} %pad_clamp_fusion.1), kind=kCustom, calls=%fused_computation.clone | custom fusion | bytes 2098176 | tf_op jit(solution)/shard_map/jit(_take)/gather | solution.py:30
  26.0 1.2 select_select_fusion.1
  27.2 0.0 all-reduce.3.cloned.1.call-update
  27.2 0.0 all-gather.11.cloned.1.call-start
  27.3 2.3 slice_select_fusion.3
  29.6 0.0 all-gather.11.cloned.1.call-update
  29.6 0.0 all-gather.13.cloned.1.call-start
  29.6 0.0 copy-done
  29.6 0.8 fusion.20
  30.4 0.0 all-gather.13.cloned.1.call-update
  30.5 0.0 all-reduce.5.cloned.1.call-start
  30.5 0.0 copy-done.1
  30.6 13.4 %all-gather.4 = bf16[1,256,256]{2,1,0:T(8,128)(2,1)S(1)} all-gather(bf16[1,32,256]{2,1,0:T(8,128)(2,1)S(1)} %get-tuple-element.71), channel_id=6, replica_groups=mesh['row'=16,'col'=8] {'col'}, dimensions={1}, use_global_device_ids=true | all-gather | bytes 147456 | tf_op jit(solution)/shard_map/all_gather | solution.py:37
  43.9 13.3 %all-gather.1 = bf16[1,256,256]{2,1,0:T(8,128)(2,1)S(1)} all-gather(bf16[1,32,256]{2,1,0:T(8,128)(2,1)S(1)} %get-tuple-element.72), channel_id=3, replica_groups=mesh['row'=16,'col'=8] {'col'}, dimensions={1}, use_global_device_ids=true | all-gather | bytes 147456 | tf_op jit(solution)/shard_map/all_gather | solution.py:37
  57.2 0.1 convert_add_fusion
  57.3 0.1 triangular_solve.107
  57.4 3.9 while.6
  57.4 0.6 fusion.28
  58.0 1.3 bitcast_dynamic-update-slice_fusion.4
  59.3 0.6 fusion.28
  59.9 1.3 bitcast_dynamic-update-slice_fusion.4
  61.3 19.7 %custom-call.4 = f32[2,128,128]{1,2,0:T(8,128)S(1)} custom-call(f32[2,128,128]{2,1,0:T(8,128)S(1)} %get-tuple-element.45), custom_call_target="InvertDiagBlocksLowerTriangular" | custom-call | tf_op jit(solution)/shard_map/jit(_solve_triangular)/triangular_solve | solution.py:40
  81.0 0.0 copy-done.3
  81.0 36.2 %all-reduce.3.cloned.1.call-done = bf16[256,2048]{1,0:T(8,128)(2,1)} async-done(((bf16[256,2048]{1,0:T(8,128)(2,1)}), bf16[256,2048]{1,0:T(8,128)(2,1)}) %all-reduce.3.cloned.1.call-update) | async-done | bytes 1048592 | tf_op jit(solution)/shard_map/psum | solution.py:39
  117.2 1.5 convert_element_type.42
  118.7 1.1 fusion.8
  119.7 1.0 convolution_subtract_fusion.1
  120.8 1.1 fusion.15
  121.8 108.2 %all-gather.11.cloned.1.call-done = bf16[4096,2048]{1,0:T(8,128)(2,1)} async-done(((bf16[256,2048]{1,0:T(8,128)(2,1)}), bf16[4096,2048]{1,0:T(8,128)(2,1)}) %all-gather.11.cloned.1.call-update) | async-done | bytes 16777232 | tf_op jit(solution)/shard_map/all_gather | solution.py:9
  230.0 9.3 %reduce_sum.24 = bf16[256,2048]{1,0:T(8,128)(2,1)S(1)} reduce(bf16[16,256,2048]{2,1,0:T(8,128)(2,1)} %bitcast.66, bf16[]{:T(256)} %constant.91.clone.1), dimensions={0}, to_apply=%region_0.1 | reduce | flops 7864320 | bytes 17825794 | tf_op jit(solution)/shard_map/reduce_sum | solution.py:10
  239.3 14.5 %scatter_fusion = bf16[3072,2048]{1,0:T(8,128)(2,1)} fusion(bf16[3072,2048]{1,0:T(8,128)(2,1)} %copy.33, s32[256]{0:T(256)S(1)} %bitcast.69, bf16[256,2048]{1,0:T(8,128)(2,1)S(1)} %reduce_sum.24), kind=kCustom, calls=%fused_computation.2 | custom fusion | bytes 3146752 | tf_op jit(solution)/shard_map/scatter | solution.py:36
  253.8 1.8 all-gather.13.cloned.1.call-done
  255.7 9.9 %fusion.1 = bf16[3072,2048]{1,0:T(8,128)(2,1)} fusion(bf16[3072,2048]{1,0:T(8,128)(2,1)} %scatter_fusion, bf16[1,256,3072]{2,1,0:T(8,128)(2,1)} %all-gather.13.cloned.1.call-done, bf16[128,2048]{1,0:T(8,128)(2,1)S(1)} %fusion.15, f32[128,2048]{1,0:T(8,128)S(1)} %fusion.8), kind=kOutput, calls=%fused_computation.11 | convolution fusion | flops 3242196992 | bytes 28311552 | tf_op jit(solution)/shard_map/dot_general | solution.py:43
  265.5 2.5 fusion.7
  268.1 8.6 %gather_fusion.1 = bf16[256,2048]{1,0:T(8,128)(2,1)S(1)} fusion(bf16[3072,2048]{1,0:T(8,128)(2,1)} %fusion.7, s32[1024]{0:T(1024)S(1)} %pad_clamp_fusion), kind=kCustom, calls=%fused_computation.1.clone | custom fusion | bytes 2098176 | tf_op jit(solution)/shard_map/jit(_take)/gather | solution.py:30
  276.6 1.2 select_select_fusion
  277.8 0.0 all-reduce.5.cloned.1.call-update
  277.8 0.0 all-gather.15.cloned.1.call-start
  277.9 2.3 slice_select_fusion.1
  280.2 0.0 all-gather.15.cloned.1.call-update
  280.2 0.3 all-gather.17.cloned.1.call-start
  280.5 0.3 all-gather.17.cloned.1.call-update
  280.8 4.1 while.7
  280.8 0.6 fusion.29
  281.5 1.3 bitcast_dynamic-update-slice_fusion.5
  282.9 0.6 fusion.29
  283.5 1.3 bitcast_dynamic-update-slice_fusion.5
  284.9 19.7 %custom-call.5 = f32[2,128,128]{1,2,0:T(8,128)S(1)} custom-call(f32[2,128,128]{2,1,0:T(8,128)S(1)} %get-tuple-element.46), custom_call_target="InvertDiagBlocksLowerTriangular" | custom-call | tf_op jit(solution)/shard_map/jit(_solve_triangular)/triangular_solve | solution.py:40
  304.6 61.0 %all-reduce.5.cloned.1.call-done = bf16[256,2048]{1,0:T(8,128)(2,1)} async-done(((bf16[256,2048]{1,0:T(8,128)(2,1)}), bf16[256,2048]{1,0:T(8,128)(2,1)}) %all-reduce.5.cloned.1.call-update) | async-done | bytes 1048592 | tf_op jit(solution)/shard_map/psum | solution.py:39
  365.5 1.5 convert_element_type.47
  367.0 1.1 fusion.5
  368.1 1.0 convolution_subtract_fusion
  369.1 1.1 fusion.13
  370.1 108.0 %all-gather.15.cloned.1.call-done = bf16[4096,2048]{1,0:T(8,128)(2,1)} async-done(((bf16[256,2048]{1,0:T(8,128)(2,1)}), bf16[4096,2048]{1,0:T(8,128)(2,1)}) %all-gather.15.cloned.1.call-update) | async-done | bytes 16777232 | tf_op jit(solution)/shard_map/all_gather | solution.py:9
  478.2 9.3 %reduce_sum.25 = bf16[256,2048]{1,0:T(8,128)(2,1)S(1)} reduce(bf16[16,256,2048]{2,1,0:T(8,128)(2,1)} %bitcast.67, bf16[]{:T(256)} %constant.91.clone.1), dimensions={0}, to_apply=%region_3.6 | reduce | flops 7864320 | bytes 17825794 | tf_op jit(solution)/shard_map/reduce_sum | solution.py:10
  487.5 14.6 %scatter_fusion.1 = bf16[3072,2048]{1,0:T(8,128)(2,1)} fusion(bf16[3072,2048]{1,0:T(8,128)(2,1)} %fusion.7, s32[256]{0:T(256)S(1)} %bitcast.68, bf16[256,2048]{1,0:T(8,128)(2,1)S(1)} %reduce_sum.25), kind=kCustom, calls=%fused_computation.3 | custom fusion | bytes 3146752 | tf_op jit(solution)/shard_map/scatter | solution.py:36
  502.0 1.6 all-gather.17.cloned.1.call-done
  503.7 9.9 %fusion = bf16[3072,2048]{1,0:T(8,128)(2,1)} fusion(bf16[3072,2048]{1,0:T(8,128)(2,1)} %scatter_fusion.1, bf16[1,256,3072]{2,1,0:T(8,128)(2,1)} %all-gather.17.cloned.1.call-done, bf16[128,2048]{1,0:T(8,128)(2,1)S(1)} %fusion.13, f32[128,2048]{1,0:T(8,128)S(1)} %fusion.5), kind=kOutput, calls=%fused_computation.9 | convolution fusion | flops 3242196992 | bytes 28311552 | tf_op jit(solution)/shard_map/dot_general | solution.py:43
  513.5 2.5 fusion.4
  (20 shorter events, 0.1 us)
Async XLA Ops:
  6.5 10.7 %copy-start.2 = (s32[2,256]{1,0:T(2,128)S(1)}, s32[2,256]{1,0:T(2,128)}, u32[]{:S(2)}) copy-start(s32[2,256]{1,0:T(2,128)} %param.16) | copy-start | bytes 6148
  6.5 110.7 %all-reduce.3.cloned.1.call-start = ((), (), s32[]{:S(2)}) async-start(), calls=%async_computation | async-start | bytes 2097152 | tf_op jit(solution)/shard_map/psum | solution.py:39
  17.3 12.4 %copy-start = (bf16[2,32,3072]{2,1,0:T(8,128)(2,1)S(1)}, bf16[2,32,3072]{2,1,0:T(8,128)(2,1)}, u32[]{:S(2)}) copy-start(bf16[2,32,3072]{2,1,0:T(8,128)(2,1)} %param.14) | copy-start | bytes 1179652
  17.3 13.3 %copy-start.1 = (bf16[2,32,256]{2,1,0:T(8,128)(2,1)S(1)}, bf16[2,32,256]{2,1,0:T(8,128)(2,1)}, u32[]{:S(2)}) copy-start(bf16[2,32,256]{2,1,0:T(8,128)(2,1)} %param.15) | copy-start | bytes 98308
  17.3 63.7 %copy-start.3 = (s32[2,256]{1,0:T(2,128)S(1)}, s32[2,256]{1,0:T(2,128)}, u32[]{:S(2)}) copy-start(s32[2,256]{1,0:T(2,128)} %param.17) | copy-start | bytes 6148
  27.2 202.8 %all-gather.11.cloned.1.call-start = ((), (), s32[]{:S(2)}) async-start(), calls=%async_computation.2 | async-start | bytes 17825792 | tf_op jit(solution)/shard_map/all_gather | solution.py:9
  29.6 226.1 %all-gather.13.cloned.1.call-start = ((), (), s32[]{:S(2)}) async-start(), calls=%async_computation.3 | async-start | bytes 1769472 | tf_op jit(solution)/shard_map/all_gather | solution.py:44
  30.5 335.1 %all-reduce.5.cloned.1.call-start = ((), (), s32[]{:S(2)}) async-start(), calls=%async_computation.1 | async-start | bytes 2097152 | tf_op jit(solution)/shard_map/psum | solution.py:39
  277.8 200.3 %all-gather.15.cloned.1.call-start = ((), (), s32[]{:S(2)}) async-start(), calls=%async_computation.4 | async-start | bytes 17825792 | tf_op jit(solution)/shard_map/all_gather | solution.py:9
  280.2 223.4 %all-gather.17.cloned.1.call-start = ((), (), s32[]{:S(2)}) async-start(), calls=%async_computation.5 | async-start | bytes 1769472 | tf_op jit(solution)/shard_map/all_gather | solution.py:44
Sparse Core Ops, SparseCore 0:
  27.3 89.8 all-reduce.2
  119.4 110.6 all-gather.10
  231.7 23.8 all-gather.12
  278.0 87.5 all-reduce.4
  367.5 110.6 all-gather.14
  479.7 23.8 all-gather.16
